TPU v7x, 256 devices: a whole 4x4x8 slice. The times are simulated.
256 devices in a mesh: blk: 32 (over x_hi, z, core), fsdp: 8 (over y, x_lo).
Axes of the slice: x: 4 (x_hi: 2, x_lo: 2; x = x_hi * 2 + x_lo), y: 4, z: 8, core: 2. Of those that a mesh axis runs over, the one named last changes fastest.
Arguments:
- params: float32 [32, 4096, 1024], P('blk', 'fsdp'), may hold values from -6 to 6
- inputs: bfloat16 [32, 7168, 4096], P('blk', 'fsdp'), may hold values from -6 to 6
- cotangent: bfloat16 [32, 7168, 1024], P('blk', 'fsdp'), may hold values from -6 to 6
- mix: int32 [32, 3], replicated, may hold values from 8 to 48, as said below
Outputs:
- new_params: float32 [32, 4096, 1024], P('blk', 'fsdp')
Inputs may be any that keep to these rules, and one draw needn't show every extreme that they name: `mix`: each row holds three positive numerators that sum to 64.
All inputs are finite; a program needn't handle non-finite values.
Results may differ from a plain program's by a relative error of at most 0.0003.
Values may be sent and summed in bfloat16 or wider, within the bound.
A program may use at most 128 MiB of HBM per device.

v0:
```python
import jax
import jax.numpy as jnp
from jax import lax
from jax.sharding import PartitionSpec as P

MIX_DENOM = 64


RATE = 0.03


def from_behind(value, axis, steps):
    count = lax.axis_size(axis)
    pairs = [(source, (source + steps) % count) for source in range(count)]
    return lax.ppermute(value, axis, pairs)


def on_device(params, inputs, cotangent, mix):
    weights = params[0]
    features = inputs[0]
    cot_local = cotangent[0]
    replica = lax.axis_index("blk")
    pick = (jnp.arange(lax.axis_size("blk")) == replica).astype(jnp.float32)
    coeff = jnp.dot(pick, mix.astype(jnp.float32), precision=lax.Precision.HIGHEST) / MIX_DENOM
    c_left = coeff[0]
    c_self = coeff[1]
    c_right = coeff[2]
    left_weights = from_behind(weights, "blk", 1)
    right_weights = from_behind(weights, "blk", -1)
    gradient = lax.psum_scatter(
        lax.dot_general(
            features, cot_local, (((0,), (0,)), ((), ())), preferred_element_type=jnp.float32
        ),
        "fsdp",
        scatter_dimension=0,
        tiled=True,
    )
    left_grads = from_behind(gradient, "blk", 1)
    right_grads = from_behind(gradient, "blk", -1)
    mixed_params = c_left * left_weights + c_self * weights + c_right * right_weights
    mixed_grads = c_left * left_grads + c_self * gradient + c_right * right_grads
    updated = mixed_params - RATE * mixed_grads
    return updated[None]


def solution(mesh):
    return jax.shard_map(
        on_device,
        mesh=mesh,
        in_specs=(P("blk", "fsdp", None), P("blk", "fsdp", None), P("blk", "fsdp", None), P()),
        out_specs=P("blk", "fsdp", None),
        check_vma=False,
    )
```

profile of v0, /device:TPU:10, one launch (start us, length us, event | category | flops | bytes accessed | tf_op | source)
XLA Modules:
  0.0 414.6 jit_solution(15558963236957865385)
XLA Ops:
  6.5 0.0 copy-start
  6.5 0.0 reduce-scatter.2.cloned.1.call-start
  6.5 1.5 copy-done
  8.0 14.4 %fusion = f32[4096,1024]{1,0:T(8,128)} fusion(bf16[1,896,4096]{2,1,0:T(8,128)(2,1)} %param.5, bf16[1,896,1024]{2,1,0:T(8,128)(2,1)S(1)} %copy-done), kind=kOutput, calls=%fused_computation | convolution fusion | flops 7516192768 | bytes 25952256 | tf_op jit(solution)/shard_map/dot_general | solution.py:31
  22.4 0.0 copy-start.1
  22.4 0.0 reduce-scatter.2.cloned.1.call-update
  22.5 0.1 collective-permute-start
  22.6 6.9 %collective-permute-start.1 = (f32[512,1024]{1,0:T(8,128)}, f32[512,1024]{1,0:T(8,128)}, u32[]{:S(2)}, u32[]{:S(2)}) collective-permute-start(f32[512,1024]{1,0:T(8,128)} %bitcast.21), channel_id=1, source_target_pairs={{0,248},{8,0},{16,8},{24,16},{32,24},{40,32},{48,40},{56,48},{64,5... | collective-permute-start | bytes 6291464 | tf_op jit(solution)/shard_map/ppermute | solution.py:15
  29.5 339.3 %reduce-scatter.2.cloned.1.call-done = f32[512,1024]{1,0:T(8,128)} async-done(((f32[4096,1024]{1,0:T(8,128)}), f32[512,1024]{1,0:T(8,128)}) %reduce-scatter.2.cloned.1.call-update) | async-done | bytes 2097168 | tf_op jit(solution)/shard_map/reduce_scatter | solution.py:30
  368.8 0.1 collective-permute-start.2
  368.9 5.2 %collective-permute-start.3 = (f32[512,1024]{1,0:T(8,128)}, f32[512,1024]{1,0:T(8,128)}, u32[]{:S(2)}, u32[]{:S(2)}) collective-permute-start(f32[512,1024]{1,0:T(8,128)} %reduce-scatter.2.cloned.1.call-done), channel_id=1, source_target_pairs={{0,248},{8,0},{16,8},{24,16},{32,24},{40,32},{48,40},{56,48},{64,5... | collective-permute-start | bytes 6291464 | tf_op jit(solution)/shard_map/ppermute | solution.py:15
  374.2 0.0 copy-done.1
  374.2 0.1 fusion.3
  374.3 0.6 fusion.9
  374.9 0.0 collective-permute-done
  374.9 0.0 collective-permute-done.1
  374.9 23.3 %collective-permute-done.2 = f32[512,1024]{1,0:T(8,128)} collective-permute-done((f32[512,1024]{1,0:T(8,128)}, f32[512,1024]{1,0:T(8,128)}, u32[]{:S(2)}, u32[]{:S(2)}) %collective-permute-start.2) | collective-permute-done | bytes 2097184 | tf_op jit(solution)/shard_map/ppermute | solution.py:15
  398.2 0.0 collective-permute-done.3
  398.2 9.5 %subtract_bitcast_fusion = f32[1,512,1024]{2,1,0:T(8,128)} fusion(f32[512,1024]{1,0:T(8,128)} %collective-permute-done.3, f32[512,1024]{1,0:T(8,128)} %reduce-scatter.2.cloned.1.call-done, f32[512,1024]{1,0:T(8,128)} %collective-permute-done.2, f32[512,1024]{1,0:T(8,128)} %collective-permute-done.1, f32[512,1024]{1,0:T(8,128)} %collective-permute-done, ...), kind=kLoop, calls=%fused_computation.2 | loop fusion | flops 6291456 | bytes 14680076 | tf_op jit(solution)/shard_map/broadcast_in_dim | solution.py:43
Async XLA Ops:
  6.5 1.5 copy-start
  6.5 362.3 %reduce-scatter.2.cloned.1.call-start = ((), (), s32[]{:S(2)}) async-start(), calls=%async_computation.1 | async-start | bytes 18874368 | tf_op jit(solution)/shard_map/reduce_scatter | solution.py:30
  22.4 351.7 %copy-start.1 = (s32[32,3]{0,1:T(4,128)S(1)}, s32[32,3]{0,1:T(4,128)}, u32[]{:S(2)}) copy-start(s32[32,3]{0,1:T(4,128)} %param.7) | copy-start | bytes 1156
  22.5 352.4 %collective-permute-start = (f32[512,1024]{1,0:T(8,128)}, f32[512,1024]{1,0:T(8,128)}, u32[]{:S(2)}, u32[]{:S(2)}) collective-permute-start(f32[512,1024]{1,0:T(8,128)} %bitcast.20), channel_id=1, source_target_pairs={{0,8},{8,16},{16,24},{24,32},{32,40},{40,48},{48,56},{56,64},{64,7... | collective-permute-start | bytes 6291464 | tf_op jit(solution)/shard_map/ppermute | solution.py:15
  22.6 352.3 %collective-permute-start.1 = (f32[512,1024]{1,0:T(8,128)}, f32[512,1024]{1,0:T(8,128)}, u32[]{:S(2)}, u32[]{:S(2)}) collective-permute-start(f32[512,1024]{1,0:T(8,128)} %bitcast.21), channel_id=1, source_target_pairs={{0,248},{8,0},{16,8},{24,16},{32,24},{40,32},{48,40},{56,48},{64,5... | collective-permute-start | bytes 6291464 | tf_op jit(solution)/shard_map/ppermute | solution.py:15
  368.8 29.4 %collective-permute-start.2 = (f32[512,1024]{1,0:T(8,128)}, f32[512,1024]{1,0:T(8,128)}, u32[]{:S(2)}, u32[]{:S(2)}) collective-permute-start(f32[512,1024]{1,0:T(8,128)} %reduce-scatter.2.cloned.1.call-done), channel_id=1, source_target_pairs={{0,8},{8,16},{16,24},{24,32},{32,40},{40,48},{48,56},{56,64},{64,7... | collective-permute-start | bytes 6291464 | tf_op jit(solution)/shard_map/ppermute | solution.py:15
  368.9 29.3 %collective-permute-start.3 = (f32[512,1024]{1,0:T(8,128)}, f32[512,1024]{1,0:T(8,128)}, u32[]{:S(2)}, u32[]{:S(2)}) collective-permute-start(f32[512,1024]{1,0:T(8,128)} %reduce-scatter.2.cloned.1.call-done), channel_id=1, source_target_pairs={{0,248},{8,0},{16,8},{24,16},{32,24},{40,32},{48,40},{56,48},{64,5... | collective-permute-start | bytes 6291464 | tf_op jit(solution)/shard_map/ppermute | solution.py:15
Sparse Core Ops, SparseCore 0:
  22.6 346.1 reduce-scatter.1
where the time goes:
time: 416 us; the launch traced here: 415 us
  waiting for transfers between devices  363 us (87%)
  matrix products  14.5 us (3%)
  between operations  13.4 us (3%)
  starting transfers between devices  12.4 us (3%)
  other arithmetic  9.54 us (2%)
    reduce_scatter x1, waiting for transfers between devices, on_device(): lax.psum_scatter(lax.dot_general(features, cot_local, (((0,), (0,)), ((),...  339 us
    ppermute x4, waiting for transfers between devices, from_behind(): return lax.ppermute(value, axis, pairs)  23.3 us
    dot_general x1, matrix products, on_device(): lax.dot_general(features, cot_local, (((0,), (0,)), ((), ())), preferred_...  14.4 us
    ppermute x4, starting transfers between devices, from_behind(): return lax.ppermute(value, axis, pairs)  12.4 us
    broadcast_in_dim x1, other arithmetic, on_device(): return updated[None]  9.54 us
  transfers between devices with their start and end apart: 5, of which 2 were waited for; matrix products, arithmetic and copies ran while one was open for 0% of the time, Pallas kernels for 0%

commit v1 on v0

v1 whole, which is shorter than its diff:
```python
import functools

import jax
import jax.numpy as jnp
from jax import lax
from jax.experimental import pallas as pl
from jax.experimental.pallas import tpu as pltpu
from jax.sharding import PartitionSpec as P

MIX_DENOM = 64
RATE = 0.03
LEVELS = 32767.0
TINY = 1e-30
MESH = pl.DeviceIdType.MESH

NY = 4
NX = 2
NSH = NY * NX
TILE = 128
R = 64
LA = 384

UP, DN = 0, 1


def message_shapes(kv):
    h, lb = R // 2, kv - LA
    return dict(
        ax=(1, NY, R, LA),
        by1=(2, 4, h, lb),
        by2=(2, 2, h, lb),
        bx=(1, 2, h, lb),
        ay1=(2, 2, h, LA),
        ay2=(2, 1, h, LA),
        u=(1, R // 16, 16, kv),
    )


def kernel(shapes, nrep, k_chunks, *refs):
    names = list(shapes)
    (params, inputs, cot_hbm, mix, out), refs = refs[:5], refs[5:]
    nm = len(names)
    sendq, sends = dict(zip(names, refs[:nm])), dict(zip(names, refs[nm : 2 * nm]))
    recvq, recvs = dict(zip(names, refs[2 * nm : 3 * nm])), dict(zip(names, refs[3 * nm : 4 * nm]))
    refs = refs[4 * nm :]
    sem_s, sem_r = dict(zip(names, refs[:nm])), dict(zip(names, refs[nm : 2 * nm]))
    part, xbuf, cot, pbuf, obuf, sem_x, sem_c, sem_p, sem_o = refs[2 * nm :]

    tokens, kv = cot.shape
    n_tiles = xbuf.shape[0]
    sub = TILE // R
    shard_rows = TILE * n_tiles
    h = R // 2
    lb = kv - LA
    A, B = slice(0, LA), slice(LA, kv)
    H = (slice(0, h), slice(h, R))

    rep = lax.axis_index("blk")
    fs = lax.axis_index("fsdp")
    y, x = fs // NX, fs % NX
    y_up, y_dn, y_far = (y + 1) % NY, (y + NY - 1) % NY, (y + 2) % NY
    dev = dict(
        up=(rep, y_up * NX + x),
        dn=(rep, y_dn * NX + x),
        x=(rep, y * NX + (1 - x)),
        right=((rep + 1) % nrep, fs),
        left=((rep + nrep - 1) % nrep, fs),
    )

    def shard(yy, xx):
        return yy * NX + xx

    def load_x(c, f):
        return pltpu.make_async_copy(
            inputs.at[0, :, pl.ds(f * shard_rows + c * TILE, TILE)],
            xbuf.at[c, :, pl.ds(f * TILE, TILE)],
            sem_x.at[c, f],
        )

    load_cot = pltpu.make_async_copy(cot_hbm.at[0], cot, sem_c)
    load_p = pltpu.make_async_copy(params.at[0], pbuf, sem_p)
    load_cot.start()
    for c in range(n_tiles):
        for f in range(NSH):
            load_x(c, f).start()
    load_p.start()

    barrier = pltpu.get_barrier_semaphore()
    for d in dev.values():
        pl.semaphore_signal(barrier, inc=1, device_id=d, device_id_type=MESH)
    pl.semaphore_wait(barrier, len(dev))

    def copies(name, d, k, to):
        return [
            pltpu.make_async_remote_copy(
                src_ref=src.at[0 if name == "u" else d, k],
                dst_ref=dst.at[d, k],
                send_sem=sem_s[name].at[d, i, k],
                recv_sem=sem_r[name].at[d, i, k],
                device_id=dev[to],
                device_id_type=MESH,
            )
            for i, (src, dst) in enumerate(
                ((sendq[name], recvq[name]), (sends[name], recvs[name]))
            )
        ]

    TO = dict(ax=("x",), bx=("x",), u=("right", "left"))

    def target(name, d):
        return TO.get(name, ("up", "dn"))[d]

    def send(name, d, k):
        for c in copies(name, d, k, target(name, d)):
            c.start()

    def arrived(name, d, k):
        for c in copies(name, d, k, target(name, d)):
            c.wait_recv()

    def sent(name, d, k):
        for c in copies(name, d, k, target(name, d)):
            c.wait_send()

    def encode(name, d, k, blocks):
        top = functools.reduce(jnp.maximum, [jnp.abs(b()) for b in blocks])
        top = jnp.maximum(jnp.max(top, axis=0, keepdims=True), TINY)
        sends[name][d, k] = top * (1.0 / LEVELS)
        inv = LEVELS / top
        for i, b in enumerate(blocks):
            sendq[name][d, k, i] = jnp.round(b() * inv).astype(jnp.int32).astype(jnp.int16)

    def decode(name, d, k, i, rows=None):
        q = recvq[name][d, k, i] if rows is None else recvq[name][d, k, i, rows]
        return q.astype(jnp.int32).astype(jnp.float32) * recvs[name][d, k]

    def at(k, f, rows, cols):
        return lambda: part[k, f, rows, cols]

    def multiply(c, j):
        lhs = xbuf[c, :, pl.ds(pl.multiple_of(j * (2 * TILE), 2 * TILE), 2 * TILE)]
        prod = lax.dot_general(
            lhs, cot[...], (((0,), (0,)), ((), ())), preferred_element_type=jnp.float32
        )
        for a in range(2):
            for i in range(sub):
                lo = a * TILE + i * R
                part[c * sub + i, 2 * j + a] = prod[lo : lo + R]

    def wait_x(c):
        for f in range(NSH):
            load_x(c, f).wait()

    def stage1(k):
        encode("ax", 0, k, [at(k, shard(yy, 1 - x), slice(0, R), A) for yy in range(NY)])
        send("ax", 0, k)
        for d, near, relay, plain in ((UP, y_up, H[1], H[0]), (DN, y_dn, H[0], H[1])):
            encode(
                "by1",
                d,
                k,
                [at(k, shard(y_far, xx), relay, B) for xx in range(NX)]
                + [at(k, shard(near, xx), plain, B) for xx in range(NX)],
            )
            send("by1", d, k)

    def stage2(k):
        for d, near, relay in ((UP, y_up, H[1]), (DN, y_dn, H[0])):
            arrived("by1", d, k)
            for xx in range(NX):
                part[k, shard(near, xx), relay, B] += decode("by1", d, k, xx)
            encode("by2", d, k, [at(k, shard(near, xx), relay, B) for xx in range(NX)])
            send("by2", d, k)
        arrived("ax", 0, k)
        for yy in range(NY):
            part[k, shard(yy, x), :, A] += decode("ax", 0, k, yy)
        for d, near, relay, plain in ((UP, y_up, H[1], H[0]), (DN, y_dn, H[0], H[1])):
            encode("ay1", d, k, [at(k, shard(y_far, x), relay, A), at(k, shard(near, x), plain, A)])
            send("ay1", d, k)

    def stage3(k):
        for d in (UP, DN):
            arrived("by2", d, k)
        for xx in (1 - x, x):
            part[k, shard(y, xx), H[0], B] += decode("by1", UP, k, 2 + xx) + decode("by2", DN, k, xx)
            part[k, shard(y, xx), H[1], B] += decode("by1", DN, k, 2 + xx) + decode("by2", UP, k, xx)
        encode("bx", 0, k, [at(k, shard(y, 1 - x), rows, B) for rows in H])
        send("bx", 0, k)
        for d, near, relay in ((UP, y_up, H[1]), (DN, y_dn, H[0])):
            arrived("ay1", d, k)
            part[k, shard(near, x), relay, A] += decode("ay1", d, k, 0)
            encode("ay2", d, k, [at(k, shard(near, x), relay, A)])
            send("ay2", d, k)

    def stage4(k):
        for d in (UP, DN):
            arrived("ay2", d, k)
        arrived("bx", 0, k)
        mine = shard(y, x)
        base = pl.multiple_of(k * R, R)
        for half in (0, 1):
            d1, d2 = ((UP, DN), (DN, UP))[half]
            rows = H[half]
            prow = pl.ds(base + half * h, h)
            g = part[k, mine, rows, A] + decode("ay1", d1, k, 1) + decode("ay2", d2, k, 0)
            part[k, mine, rows, A] = pbuf[prow, A] - RATE * g
            g = part[k, mine, rows, B] + decode("bx", 0, k, half)
            part[k, mine, rows, B] = pbuf[prow, B] - RATE * g
        n = R // 16
        encode("u", 0, k, [at(k, mine, slice(16 * i, 16 * i + 16), slice(0, kv)) for i in range(n)])
        for d in (0, 1):
            send("u", d, k)

    c_left = mix[rep, 0].astype(jnp.float32) * (1.0 / MIX_DENOM)
    c_self = mix[rep, 1].astype(jnp.float32) * (1.0 / MIX_DENOM)
    c_right = mix[rep, 2].astype(jnp.float32) * (1.0 / MIX_DENOM)

    def store(k):
        base = pl.multiple_of(k * R, R)
        return pltpu.make_async_copy(obuf.at[k], out.at[0, pl.ds(base, R)], sem_o.at[k])

    def stage5(k):
        for d in (0, 1):
            arrived("u", d, k)
        mine = shard(y, x)
        for i in range(R // 16):
            rows = slice(16 * i, 16 * i + 16)
            obuf[k, rows] = (
                c_left * decode("u", 0, k, i)
                + c_self * part[k, mine, rows]
                + c_right * decode("u", 1, k, i)
            )
        store(k).start()

    load_cot.wait()
    wait_x(0)
    per_tile = NSH // 2

    @pl.loop(0, per_tile)
    def _(j):
        multiply(0, j)

    share = per_tile // sub

    @pl.loop(0, k_chunks + 4)
    def _(s):
        @pl.when(s < k_chunks)
        def _():
            stage1(s)

        c = s // sub + 1

        @pl.when(c < n_tiles)
        def _():
            @pl.when(s % sub == 0)
            def _():
                for f in range(NSH):
                    load_x(c, f).wait()

            @pl.loop(0, share)
            def _(j):
                multiply(c, (s % sub) * share + j)

        @pl.when(s == 0)
        def _():
            load_p.wait()

        for lag, stage in ((1, stage2), (2, stage3), (3, stage4), (4, stage5)):

            @pl.when((s >= lag) & (s < k_chunks + lag))
            def _(lag=lag, stage=stage):
                stage(s - lag)

    @pl.loop(0, k_chunks)
    def _(k):
        for name, shape in shapes.items():
            for d in range(2 if name == "u" else shape[0]):
                sent(name, d, k)
        store(k).wait()


def on_device(nrep, params, inputs, cotangent, mix):
    _, tokens, width = inputs.shape
    kv = cotangent.shape[-1]
    rows = params.shape[1]
    n_tiles = rows // TILE
    k_chunks = rows // R
    shapes = message_shapes(kv)
    names = list(shapes)
    landing = {n: (2 if n == "u" else s[0],) + s[1:] for n, s in shapes.items()}

    def data(table):
        return [pltpu.VMEM((s[0], k_chunks) + s[1:], jnp.int16) for s in table.values()]

    def scales(table):
        return [pltpu.VMEM((s[0], k_chunks, 1, s[3]), jnp.float32) for s in table.values()]

    sems = [pltpu.SemaphoreType.DMA((landing[n][0], 2, k_chunks)) for n in names]
    scratch = (
        data(shapes)
        + scales(shapes)
        + data(landing)
        + scales(landing)
        + sems
        + sems
        + [
            pltpu.VMEM((k_chunks, NSH, R, kv), jnp.float32),
            pltpu.VMEM((n_tiles, tokens, NSH * TILE), jnp.bfloat16),
            pltpu.VMEM((tokens, kv), jnp.bfloat16),
            pltpu.VMEM((rows, kv), jnp.float32),
            pltpu.VMEM((k_chunks, R, kv), jnp.float32),
            pltpu.SemaphoreType.DMA((n_tiles, NSH)),
            pltpu.SemaphoreType.DMA,
            pltpu.SemaphoreType.DMA,
            pltpu.SemaphoreType.DMA((k_chunks,)),
        ]
    )
    hbm = pl.BlockSpec(memory_space=pl.ANY)
    return pl.pallas_call(
        functools.partial(kernel, shapes, nrep, k_chunks),
        out_shape=jax.ShapeDtypeStruct(params.shape, jnp.float32),
        in_specs=[hbm, hbm, hbm, pl.BlockSpec(memory_space=pltpu.SMEM)],
        out_specs=hbm,
        scratch_shapes=scratch,
        compiler_params=pltpu.CompilerParams(
            collective_id=0, has_side_effects=True, vmem_limit_bytes=62 << 20
        ),
        name="gossip_step",
    )(params, inputs, cotangent, mix)


def solution(mesh):
    return jax.shard_map(
        functools.partial(on_device, mesh.shape["blk"]),
        mesh=mesh,
        in_specs=(P("blk", "fsdp", None), P("blk", "fsdp", None), P("blk", "fsdp", None), P()),
        out_specs=P("blk", "fsdp", None),
        check_vma=False,
    )
```

time: 416 us -> 89.2 us (0.21)
  the two profiles are of different devices: /device:TPU:10 before, /device:TPU:2 now
where the time goes in v1:
time: 89.2 us; the launch traced here: 89 us
  Pallas kernels  84.5 us (95%)
  local copies, waits for them, and re-layouts  4.53 us (5%)
    pallas_call x1, Pallas kernels, on_device(): pl.pallas_call(functools.partial(kernel, shapes, nrep, k_chunks), out_sha...  84.5 us
    unnamed x2, local copies, waits for them, and re-layouts  4.53 us

profile of v1, /device:TPU:2, one launch (start us, length us, event | category | flops | bytes accessed | tf_op | source)
XLA Modules:
  0.0 89.0 jit_solution(904063506494979657)
XLA Ops:
  0.0 1.4 %copy.5.refs_3_ = s32[32,3]{1,0:T(8,128)} copy(s32[32,3]{0,1:T(4,128)} %param.7) | data formatting | bytes 768 | tf_op args[3]
  1.4 84.5 %gossip_step.1 = f32[1,512,1024]{2,1,0:T(8,128)} custom-call(f32[1,512,1024]{2,1,0:T(8,128)} %refs_0_.1, bf16[1,896,4096]{2,1,0:T(8,128)(2,1)} %refs_1_.1, bf16[1,896,1024]{2,1,0:T(8,128)(2,1)} %refs_2_.1, s32[32,3]{1,0:T(8,128)} %copy.5.refs_3_), custom_call_target="tpu_custom_call" | custom-call | tf_op jit(solution)/shard_map/gossip_step/pallas_call | solution.py:319
  85.9 3.2 %copy.7 = f32[1,512,1024]{2,1,0:T(8,128)} copy(f32[1,512,1024]{2,1,0:T(8,128)} %gossip_step.1) | data formatting | bytes 4194304

commit v2 on v1

--- a/solution.py
+++ b/solution.py
@@ -21,6 +21,7 @@
 LA = 384
 
 UP, DN = 0, 1
+CUT = 256
 
 
 def message_shapes(kv):
@@ -44,7 +45,7 @@
     recvq, recvs = dict(zip(names, refs[2 * nm : 3 * nm])), dict(zip(names, refs[3 * nm : 4 * nm]))
     refs = refs[4 * nm :]
     sem_s, sem_r = dict(zip(names, refs[:nm])), dict(zip(names, refs[nm : 2 * nm]))
-    part, xbuf, cot, pbuf, obuf, sem_x, sem_c, sem_p, sem_o = refs[2 * nm :]
+    part, xbuf, cot, pbuf, mbuf, sem_x, sem_c, sem_p, sem_m = refs[2 * nm :]
 
     tokens, kv = cot.shape
     n_tiles = xbuf.shape[0]
@@ -72,23 +73,33 @@
 
     def load_x(c, f):
         return pltpu.make_async_copy(
-            inputs.at[0, :, pl.ds(f * shard_rows + c * TILE, TILE)],
-            xbuf.at[c, :, pl.ds(f * TILE, TILE)],
+            inputs.at[0, :, pl.ds(pl.multiple_of(f * shard_rows + c * TILE, TILE), TILE)],
+            xbuf.at[c, :, pl.ds(pl.multiple_of(f * TILE, TILE), TILE)],
             sem_x.at[c, f],
         )
 
-    load_cot = pltpu.make_async_copy(cot_hbm.at[0], cot, sem_c)
+    early, late = slice(CUT, kv), slice(0, CUT)
+
+    def load_cot(i, cols):
+        return pltpu.make_async_copy(cot_hbm.at[0, :, cols], cot.at[:, cols], sem_c.at[i])
+
     load_p = pltpu.make_async_copy(params.at[0], pbuf, sem_p)
-    load_cot.start()
-    for c in range(n_tiles):
-        for f in range(NSH):
-            load_x(c, f).start()
-    load_p.start()
+    load_mix = pltpu.make_async_copy(mix, mbuf, sem_m)
+    def tile_x(yy):
+        return [load_x(0, shard(yy, xx)) for xx in range(NX)]
+
+    load_cot(0, early).start()
+    for yy in (y_far, y_up):
+        for load in tile_x(yy):
+            load.start()
+    for yy in (y_dn, y):
+        for load in tile_x(yy):
+            load.start()
+    load_cot(1, late).start()
 
     barrier = pltpu.get_barrier_semaphore()
     for d in dev.values():
         pl.semaphore_signal(barrier, inc=1, device_id=d, device_id_type=MESH)
-    pl.semaphore_wait(barrier, len(dev))
 
     def copies(name, d, k, to):
         return [
@@ -137,32 +148,37 @@
     def at(k, f, rows, cols):
         return lambda: part[k, f, rows, cols]
 
-    def multiply(c, j):
+    def multiply(c, j, cols=slice(0, kv)):
         lhs = xbuf[c, :, pl.ds(pl.multiple_of(j * (2 * TILE), 2 * TILE), 2 * TILE)]
         prod = lax.dot_general(
-            lhs, cot[...], (((0,), (0,)), ((), ())), preferred_element_type=jnp.float32
+            lhs, cot[:, cols], (((0,), (0,)), ((), ())), preferred_element_type=jnp.float32
         )
         for a in range(2):
             for i in range(sub):
                 lo = a * TILE + i * R
-                part[c * sub + i, 2 * j + a] = prod[lo : lo + R]
-
-    def wait_x(c):
-        for f in range(NSH):
-            load_x(c, f).wait()
-
-    def stage1(k):
+                part[c * sub + i, 2 * j + a, :, cols] = prod[lo : lo + R]
+
+    BY1 = {UP: (y_up, H[1], H[0]), DN: (y_dn, H[0], H[1])}
+
+    def first_y(k, d):
+        near, relay, plain = BY1[d]
+        encode(
+            "by1",
+            d,
+            k,
+            [at(k, shard(y_far, xx), relay, B) for xx in range(NX)]
+            + [at(k, shard(near, xx), plain, B) for xx in range(NX)],
+        )
+        send("by1", d, k)
+
+    def first_x(k):
         encode("ax", 0, k, [at(k, shard(yy, 1 - x), slice(0, R), A) for yy in range(NY)])
         send("ax", 0, k)
-        for d, near, relay, plain in ((UP, y_up, H[1], H[0]), (DN, y_dn, H[0], H[1])):
-            encode(
-                "by1",
-                d,
-                k,
-                [at(k, shard(y_far, xx), relay, B) for xx in range(NX)]
-                + [at(k, shard(near, xx), plain, B) for xx in range(NX)],
-            )
-            send("by1", d, k)
+
+    def stage1(k):
+        first_x(k)
+        for d in (UP, DN):
+            first_y(k, d)
 
     def stage2(k):
         for d, near, relay in ((UP, y_up, H[1]), (DN, y_dn, H[0])):
@@ -211,40 +227,55 @@
         for d in (0, 1):
             send("u", d, k)
 
-    c_left = mix[rep, 0].astype(jnp.float32) * (1.0 / MIX_DENOM)
-    c_self = mix[rep, 1].astype(jnp.float32) * (1.0 / MIX_DENOM)
-    c_right = mix[rep, 2].astype(jnp.float32) * (1.0 / MIX_DENOM)
-
-    def store(k):
-        base = pl.multiple_of(k * R, R)
-        return pltpu.make_async_copy(obuf.at[k], out.at[0, pl.ds(base, R)], sem_o.at[k])
-
     def stage5(k):
         for d in (0, 1):
             arrived("u", d, k)
         mine = shard(y, x)
+        column = lax.broadcasted_iota(jnp.int32, mbuf.shape, 1) == rep
+        coeff = jnp.where(column, mbuf[...].astype(jnp.float32) * (1.0 / MIX_DENOM), 0.0)
+        coeff = jnp.sum(coeff, axis=1, keepdims=True)
+        c_left, c_self, c_right = coeff[0:1], coeff[1:2], coeff[2:3]
         for i in range(R // 16):
             rows = slice(16 * i, 16 * i + 16)
-            obuf[k, rows] = (
+            out[0, pl.ds(pl.multiple_of(k * R + 16 * i, 16), 16)] = (
                 c_left * decode("u", 0, k, i)
                 + c_self * part[k, mine, rows]
                 + c_right * decode("u", 1, k, i)
             )
-        store(k).start()
-
-    load_cot.wait()
-    wait_x(0)
+
+    load_cot(0, early).wait()
+    for yy in (y_far, y_up):
+        for load in tile_x(yy):
+            load.wait()
+        multiply(0, yy, early)
+    pl.semaphore_wait(barrier, len(dev))
+    first_y(0, UP)
+    for yy in (y_dn, y):
+        for load in tile_x(yy):
+            load.wait()
+    load_cot(1, late).wait()
+    for c in range(1, n_tiles):
+        for f in range(NSH):
+            load_x(c, f).start()
+    load_p.start()
+    load_mix.start()
+    multiply(0, y_dn, early)
+    first_y(0, DN)
+
     per_tile = NSH // 2
 
     @pl.loop(0, per_tile)
     def _(j):
-        multiply(0, j)
+        multiply(0, j, late)
+
+    multiply(0, y, early)
+    first_x(0)
 
     share = per_tile // sub
 
     @pl.loop(0, k_chunks + 4)
     def _(s):
-        @pl.when(s < k_chunks)
+        @pl.when((s >= 1) & (s < k_chunks))
         def _():
             stage1(s)
 
@@ -264,6 +295,7 @@
         @pl.when(s == 0)
         def _():
             load_p.wait()
+            load_mix.wait()
 
         for lag, stage in ((1, stage2), (2, stage3), (3, stage4), (4, stage5)):
 
@@ -276,7 +308,6 @@
         for name, shape in shapes.items():
             for d in range(2 if name == "u" else shape[0]):
                 sent(name, d, k)
-        store(k).wait()
 
 
 def on_device(nrep, params, inputs, cotangent, mix):
@@ -308,25 +339,25 @@
             pltpu.VMEM((n_tiles, tokens, NSH * TILE), jnp.bfloat16),
             pltpu.VMEM((tokens, kv), jnp.bfloat16),
             pltpu.VMEM((rows, kv), jnp.float32),
-            pltpu.VMEM((k_chunks, R, kv), jnp.float32),
+            pltpu.VMEM(mix.shape[::-1], mix.dtype),
             pltpu.SemaphoreType.DMA((n_tiles, NSH)),
+            pltpu.SemaphoreType.DMA((2,)),
             pltpu.SemaphoreType.DMA,
             pltpu.SemaphoreType.DMA,
-            pltpu.SemaphoreType.DMA((k_chunks,)),
         ]
     )
     hbm = pl.BlockSpec(memory_space=pl.ANY)
     return pl.pallas_call(
         functools.partial(kernel, shapes, nrep, k_chunks),
-        out_shape=jax.ShapeDtypeStruct(params.shape, jnp.float32),
-        in_specs=[hbm, hbm, hbm, pl.BlockSpec(memory_space=pltpu.SMEM)],
-        out_specs=hbm,
+        out_shape=pltpu.VMEM(params.shape, jnp.float32),
+        in_specs=[hbm, hbm, hbm, hbm],
+        out_specs=pl.BlockSpec(memory_space=pltpu.VMEM),
         scratch_shapes=scratch,
         compiler_params=pltpu.CompilerParams(
-            collective_id=0, has_side_effects=True, vmem_limit_bytes=62 << 20
+            collective_id=0, has_side_effects=True, vmem_limit_bytes=61 << 20
         ),
         name="gossip_step",
-    )(params, inputs, cotangent, mix)
+    )(params, inputs, cotangent, mix.T)
 
 
 def solution(mesh):

time: 89.2 us -> 83.2 us (0.933)
  the two profiles are of different devices: /device:TPU:2 before, /device:TPU:8 now
where the time goes in v2:
time: 83.2 us; the launch traced here: 83.1 us
  Pallas kernels  81.8 us (98%)
  local copies, waits for them, and re-layouts  1.32 us (2%)
    pallas_call x1, Pallas kernels, on_device(): pl.pallas_call(functools.partial(kernel, shapes, nrep, k_chunks), out_sha...  81.8 us

profile of v2, /device:TPU:8, one launch (start us, length us, event | category | flops | bytes accessed | tf_op | source)
XLA Modules:
  0.0 83.1 jit_solution(17131519877906981062)
XLA Ops:
  0.0 81.8 %gossip_step.1 = f32[1,512,1024]{2,1,0:T(8,128)S(1)} custom-call(f32[1,512,1024]{2,1,0:T(8,128)} %refs_0_.1, bf16[1,896,4096]{2,1,0:T(8,128)(2,1)} %refs_1_.1, bf16[1,896,1024]{2,1,0:T(8,128)(2,1)} %refs_2_.1, s32[3,32]{1,0:T(4,128)} %bitcast.1), custom_call_target="tpu_custom_call" | custom-call | tf_op jit(solution)/shard_map/gossip_step/pallas_call | solution.py:350
  81.8 1.3 %copy.6 = f32[1,512,1024]{2,1,0:T(8,128)} copy(f32[1,512,1024]{2,1,0:T(8,128)S(1)} %gossip_step.1) | data formatting | bytes 4194304

commit v3 on v2

--- a/solution.py
+++ b/solution.py
@@ -17,7 +17,7 @@
 NX = 2
 NSH = NY * NX
 TILE = 128
-R = 64
+R = 128
 LA = 384
 
 UP, DN = 0, 1
@@ -29,9 +29,8 @@
     return dict(
         ax=(1, NY, R, LA),
         by1=(2, 4, h, lb),
-        by2=(2, 2, h, lb),
+        mid=(2, 2, h, kv),
         bx=(1, 2, h, lb),
-        ay1=(2, 2, h, LA),
         ay2=(2, 1, h, LA),
         u=(1, R // 16, 16, kv),
     )
@@ -133,17 +132,19 @@
         for c in copies(name, d, k, target(name, d)):
             c.wait_send()
 
-    def encode(name, d, k, blocks):
+    def encode(name, d, k, blocks, cols=None):
         top = functools.reduce(jnp.maximum, [jnp.abs(b()) for b in blocks])
         top = jnp.maximum(jnp.max(top, axis=0, keepdims=True), TINY)
-        sends[name][d, k] = top * (1.0 / LEVELS)
+        cols = slice(0, top.shape[1]) if cols is None else cols
+        sends[name][d, k, :, cols] = top * (1.0 / LEVELS)
         inv = LEVELS / top
         for i, b in enumerate(blocks):
-            sendq[name][d, k, i] = jnp.round(b() * inv).astype(jnp.int32).astype(jnp.int16)
-
-    def decode(name, d, k, i, rows=None):
-        q = recvq[name][d, k, i] if rows is None else recvq[name][d, k, i, rows]
-        return q.astype(jnp.int32).astype(jnp.float32) * recvs[name][d, k]
+            sendq[name][d, k, i, :, cols] = jnp.round(b() * inv).astype(jnp.int32).astype(jnp.int16)
+
+    def decode(name, d, k, i, cols=None):
+        cols = slice(0, recvs[name].shape[-1]) if cols is None else cols
+        q = recvq[name][d, k, i, :, cols].astype(jnp.int32).astype(jnp.float32)
+        return q * recvs[name][d, k, :, cols]
 
     def at(k, f, rows, cols):
         return lambda: part[k, f, rows, cols]
@@ -181,30 +182,32 @@
             first_y(k, d)
 
     def stage2(k):
-        for d, near, relay in ((UP, y_up, H[1]), (DN, y_dn, H[0])):
+        for d in (UP, DN):
+            near, relay, _ = BY1[d]
             arrived("by1", d, k)
             for xx in range(NX):
                 part[k, shard(near, xx), relay, B] += decode("by1", d, k, xx)
-            encode("by2", d, k, [at(k, shard(near, xx), relay, B) for xx in range(NX)])
-            send("by2", d, k)
+            encode("mid", d, k, [at(k, shard(near, xx), relay, B) for xx in range(NX)], B)
         arrived("ax", 0, k)
         for yy in range(NY):
             part[k, shard(yy, x), :, A] += decode("ax", 0, k, yy)
-        for d, near, relay, plain in ((UP, y_up, H[1], H[0]), (DN, y_dn, H[0], H[1])):
-            encode("ay1", d, k, [at(k, shard(y_far, x), relay, A), at(k, shard(near, x), plain, A)])
-            send("ay1", d, k)
+        for d in (UP, DN):
+            near, relay, plain = BY1[d]
+            blocks = [at(k, shard(y_far, x), relay, A), at(k, shard(near, x), plain, A)]
+            encode("mid", d, k, blocks, A)
+            send("mid", d, k)
 
     def stage3(k):
         for d in (UP, DN):
-            arrived("by2", d, k)
+            arrived("mid", d, k)
         for xx in (1 - x, x):
-            part[k, shard(y, xx), H[0], B] += decode("by1", UP, k, 2 + xx) + decode("by2", DN, k, xx)
-            part[k, shard(y, xx), H[1], B] += decode("by1", DN, k, 2 + xx) + decode("by2", UP, k, xx)
+            part[k, shard(y, xx), H[0], B] += decode("by1", UP, k, 2 + xx) + decode("mid", DN, k, xx, B)
+            part[k, shard(y, xx), H[1], B] += decode("by1", DN, k, 2 + xx) + decode("mid", UP, k, xx, B)
         encode("bx", 0, k, [at(k, shard(y, 1 - x), rows, B) for rows in H])
         send("bx", 0, k)
-        for d, near, relay in ((UP, y_up, H[1]), (DN, y_dn, H[0])):
-            arrived("ay1", d, k)
-            part[k, shard(near, x), relay, A] += decode("ay1", d, k, 0)
+        for d in (UP, DN):
+            near, relay, _ = BY1[d]
+            part[k, shard(near, x), relay, A] += decode("mid", d, k, 0, A)
             encode("ay2", d, k, [at(k, shard(near, x), relay, A)])
             send("ay2", d, k)
 
@@ -218,14 +221,18 @@
             d1, d2 = ((UP, DN), (DN, UP))[half]
             rows = H[half]
             prow = pl.ds(base + half * h, h)
-            g = part[k, mine, rows, A] + decode("ay1", d1, k, 1) + decode("ay2", d2, k, 0)
+            g = part[k, mine, rows, A] + decode("mid", d1, k, 1, A) + decode("ay2", d2, k, 0)
             part[k, mine, rows, A] = pbuf[prow, A] - RATE * g
             g = part[k, mine, rows, B] + decode("bx", 0, k, half)
             part[k, mine, rows, B] = pbuf[prow, B] - RATE * g
         n = R // 16
         encode("u", 0, k, [at(k, mine, slice(16 * i, 16 * i + 16), slice(0, kv)) for i in range(n)])
-        for d in (0, 1):
-            send("u", d, k)
+        for core, order in ((0, (1, 0)), (1, (0, 1))):
+
+            @pl.when(rep % 2 == core)
+            def _(order=order):
+                for d in order:
+                    send("u", d, k)
 
     def stage5(k):
         for d in (0, 1):
@@ -244,31 +251,35 @@
             )
 
     load_cot(0, early).wait()
-    for yy in (y_far, y_up):
+    per_tile = NSH // 2
+
+    @pl.loop(0, NY)
+    def _(i):
+        yy = (y + 2 - i + 3 * (i // 2) - 2 * (i // 3) + NY) % NY
         for load in tile_x(yy):
             load.wait()
         multiply(0, yy, early)
-    pl.semaphore_wait(barrier, len(dev))
-    first_y(0, UP)
-    for yy in (y_dn, y):
-        for load in tile_x(yy):
-            load.wait()
+
+        @pl.when(i == 1)
+        def _():
+            pl.semaphore_wait(barrier, len(dev))
+            first_y(0, UP)
+
+        @pl.when(i == 2)
+        def _():
+            for c in range(1, n_tiles):
+                for f in range(NSH):
+                    load_x(c, f).start()
+            load_p.start()
+            load_mix.start()
+            first_y(0, DN)
+
     load_cot(1, late).wait()
-    for c in range(1, n_tiles):
-        for f in range(NSH):
-            load_x(c, f).start()
-    load_p.start()
-    load_mix.start()
-    multiply(0, y_dn, early)
-    first_y(0, DN)
-
-    per_tile = NSH // 2
 
     @pl.loop(0, per_tile)
     def _(j):
         multiply(0, j, late)
 
-    multiply(0, y, early)
     first_x(0)
 
     share = per_tile // sub

time: 83.2 us -> 81.3 us (0.977)
  the two profiles are of different devices: /device:TPU:8 before, /device:TPU:10 now
where the time goes in v3:
time: 81.3 us
  Pallas kernels  79.9 us (98%)
  local copies, waits for them, and re-layouts  1.32 us (2%)
    pallas_call x1, Pallas kernels, on_device(): pl.pallas_call(functools.partial(kernel, shapes, nrep, k_chunks), out_sha...  79.9 us

profile of v3, /device:TPU:10, one launch (start us, length us, event | category | flops | bytes accessed | tf_op | source)
XLA Modules:
  0.0 81.3 jit_solution(10202439514545203698)
XLA Ops:
  0.0 79.9 %gossip_step.1 = f32[1,512,1024]{2,1,0:T(8,128)S(1)} custom-call(f32[1,512,1024]{2,1,0:T(8,128)} %refs_0_.1, bf16[1,896,4096]{2,1,0:T(8,128)(2,1)} %refs_1_.1, bf16[1,896,1024]{2,1,0:T(8,128)(2,1)} %refs_2_.1, s32[3,32]{1,0:T(4,128)} %bitcast.1), custom_call_target="tpu_custom_call" | custom-call | tf_op jit(solution)/shard_map/gossip_step/pallas_call | solution.py:361
  79.9 1.3 %copy.6 = f32[1,512,1024]{2,1,0:T(8,128)} copy(f32[1,512,1024]{2,1,0:T(8,128)S(1)} %gossip_step.1) | data formatting | bytes 4194304

commit v4 on v3

--- a/solution.py
+++ b/solution.py
@@ -21,6 +21,7 @@
 LA = 384
 
 UP, DN = 0, 1
+U = ("u0", "u1")
 CUT = 256
 
 
@@ -32,7 +33,8 @@
         mid=(2, 2, h, kv),
         bx=(1, 2, h, lb),
         ay2=(2, 1, h, LA),
-        u=(1, R // 16, 16, kv),
+        u0=(1, h // 16, 16, kv),
+        u1=(1, h // 16, 16, kv),
     )
 
 
@@ -103,7 +105,7 @@
     def copies(name, d, k, to):
         return [
             pltpu.make_async_remote_copy(
-                src_ref=src.at[0 if name == "u" else d, k],
+                src_ref=src.at[0 if name in U else d, k],
                 dst_ref=dst.at[d, k],
                 send_sem=sem_s[name].at[d, i, k],
                 recv_sem=sem_r[name].at[d, i, k],
@@ -115,7 +117,7 @@
             )
         ]
 
-    TO = dict(ax=("x",), bx=("x",), u=("right", "left"))
+    TO = dict(ax=("x",), bx=("x",), u0=("right", "left"), u1=("right", "left"))
 
     def target(name, d):
         return TO.get(name, ("up", "dn"))[d]
@@ -182,27 +184,35 @@
             first_y(k, d)
 
     def stage2(k):
+        def add_x(yy):
+            part[k, shard(yy, x), :, A] += decode("ax", 0, k, yy)
+
         for d in (UP, DN):
-            near, relay, _ = BY1[d]
+            near, relay, plain = BY1[d]
             arrived("by1", d, k)
             for xx in range(NX):
                 part[k, shard(near, xx), relay, B] += decode("by1", d, k, xx)
             encode("mid", d, k, [at(k, shard(near, xx), relay, B) for xx in range(NX)], B)
-        arrived("ax", 0, k)
-        for yy in range(NY):
-            part[k, shard(yy, x), :, A] += decode("ax", 0, k, yy)
-        for d in (UP, DN):
-            near, relay, plain = BY1[d]
+            if d == UP:
+                arrived("ax", 0, k)
+                add_x(y_far)
+            add_x(near)
             blocks = [at(k, shard(y_far, x), relay, A), at(k, shard(near, x), plain, A)]
             encode("mid", d, k, blocks, A)
             send("mid", d, k)
+        add_x(y)
 
     def stage3(k):
+        def add_y(xx):
+            for up, rows in ((0, H[1]), (1, H[0])):
+                one, two = ((DN, UP), (UP, DN))[up]
+                part[k, shard(y, xx), rows, B] += decode("by1", one, k, 2 + xx) + decode(
+                    "mid", two, k, xx, B
+                )
+
         for d in (UP, DN):
             arrived("mid", d, k)
-        for xx in (1 - x, x):
-            part[k, shard(y, xx), H[0], B] += decode("by1", UP, k, 2 + xx) + decode("mid", DN, k, xx, B)
-            part[k, shard(y, xx), H[1], B] += decode("by1", DN, k, 2 + xx) + decode("mid", UP, k, xx, B)
+        add_y(1 - x)
         encode("bx", 0, k, [at(k, shard(y, 1 - x), rows, B) for rows in H])
         send("bx", 0, k)
         for d in (UP, DN):
@@ -210,45 +220,42 @@
             part[k, shard(near, x), relay, A] += decode("mid", d, k, 0, A)
             encode("ay2", d, k, [at(k, shard(near, x), relay, A)])
             send("ay2", d, k)
+        add_y(x)
 
     def stage4(k):
-        for d in (UP, DN):
-            arrived("ay2", d, k)
         arrived("bx", 0, k)
         mine = shard(y, x)
         base = pl.multiple_of(k * R, R)
-        for half in (0, 1):
+        for half, name in enumerate(U):
             d1, d2 = ((UP, DN), (DN, UP))[half]
+            arrived("ay2", d2, k)
             rows = H[half]
             prow = pl.ds(base + half * h, h)
             g = part[k, mine, rows, A] + decode("mid", d1, k, 1, A) + decode("ay2", d2, k, 0)
             part[k, mine, rows, A] = pbuf[prow, A] - RATE * g
             g = part[k, mine, rows, B] + decode("bx", 0, k, half)
             part[k, mine, rows, B] = pbuf[prow, B] - RATE * g
-        n = R // 16
-        encode("u", 0, k, [at(k, mine, slice(16 * i, 16 * i + 16), slice(0, kv)) for i in range(n)])
-        for core, order in ((0, (1, 0)), (1, (0, 1))):
-
-            @pl.when(rep % 2 == core)
-            def _(order=order):
-                for d in order:
-                    send("u", d, k)
+            starts = [half * h + 16 * i for i in range(h // 16)]
+            encode(name, 0, k, [at(k, mine, slice(i, i + 16), slice(0, kv)) for i in starts])
+            for d in (0, 1):
+                send(name, d, k)
 
     def stage5(k):
-        for d in (0, 1):
-            arrived("u", d, k)
         mine = shard(y, x)
         column = lax.broadcasted_iota(jnp.int32, mbuf.shape, 1) == rep
         coeff = jnp.where(column, mbuf[...].astype(jnp.float32) * (1.0 / MIX_DENOM), 0.0)
         coeff = jnp.sum(coeff, axis=1, keepdims=True)
         c_left, c_self, c_right = coeff[0:1], coeff[1:2], coeff[2:3]
-        for i in range(R // 16):
-            rows = slice(16 * i, 16 * i + 16)
-            out[0, pl.ds(pl.multiple_of(k * R + 16 * i, 16), 16)] = (
-                c_left * decode("u", 0, k, i)
-                + c_self * part[k, mine, rows]
-                + c_right * decode("u", 1, k, i)
-            )
+        for half, name in enumerate(U):
+            for d in (0, 1):
+                arrived(name, d, k)
+            for i in range(h // 16):
+                row = half * h + 16 * i
+                out[0, pl.ds(pl.multiple_of(k * R + row, 16), 16)] = (
+                    c_left * decode(name, 0, k, i)
+                    + c_self * part[k, mine, row : row + 16]
+                    + c_right * decode(name, 1, k, i)
+                )
 
     load_cot(0, early).wait()
     per_tile = NSH // 2
@@ -317,7 +324,7 @@
     @pl.loop(0, k_chunks)
     def _(k):
         for name, shape in shapes.items():
-            for d in range(2 if name == "u" else shape[0]):
+            for d in range(2 if name in U else shape[0]):
                 sent(name, d, k)
 
 
@@ -329,7 +336,7 @@
     k_chunks = rows // R
     shapes = message_shapes(kv)
     names = list(shapes)
-    landing = {n: (2 if n == "u" else s[0],) + s[1:] for n, s in shapes.items()}
+    landing = {n: (2 if n in U else s[0],) + s[1:] for n, s in shapes.items()}
 
     def data(table):
         return [pltpu.VMEM((s[0], k_chunks) + s[1:], jnp.int16) for s in table.values()]

time: 81.3 us -> 81.5 us (level)
  no operation moved by 1% of the time
where the time goes in v4:
time: 81.5 us; the launch traced here: 81.4 us
  Pallas kernels  80.1 us (98%)
  local copies, waits for them, and re-layouts  1.32 us (2%)
    pallas_call x1, Pallas kernels, on_device(): pl.pallas_call(functools.partial(kernel, shapes, nrep, k_chunks), out_sha...  80.1 us

profile of v4, /device:TPU:10, one launch (start us, length us, event | category | flops | bytes accessed | tf_op | source)
XLA Modules:
  0.0 81.4 jit_solution(12102700982142322937)
XLA Ops:
  0.0 80.1 %gossip_step.1 = f32[1,512,1024]{2,1,0:T(8,128)S(1)} custom-call(f32[1,512,1024]{2,1,0:T(8,128)} %refs_0_.1, bf16[1,896,4096]{2,1,0:T(8,128)(2,1)} %refs_1_.1, bf16[1,896,1024]{2,1,0:T(8,128)(2,1)} %refs_2_.1, s32[3,32]{1,0:T(4,128)} %bitcast.1), custom_call_target="tpu_custom_call" | custom-call | tf_op jit(solution)/shard_map/gossip_step/pallas_call | solution.py:368
  80.1 1.3 %copy.6 = f32[1,512,1024]{2,1,0:T(8,128)} copy(f32[1,512,1024]{2,1,0:T(8,128)S(1)} %gossip_step.1) | data formatting | bytes 4194304
